TPU v7x, 512 devices: a whole 4x8x8 slice. The times are simulated.
512 devices in a mesh: req: 64 (over x, y, core), tp: 8 (over z).
Axes of the slice: x: 4, y: 8, z: 8, core: 2. Of those that a mesh axis runs over, the one named last changes fastest.
Arguments:
- queries: bfloat16 [64, 28, 4096], P('req', None, 'tp'), may hold values from -25 to 25
- tree_kv: bfloat16 [64, 28, 2048], P('req', None, 'tp'), may hold values from -4 to 4
- tree_parent: int32 [64, 28], P('req'), may hold values from -1 to 26, as said below
- accepted_path: int32 [64, 8], replicated, may hold values from -1 to 27, as said below
- cache_kv: bfloat16 [192, 256, 2048], P('req', None, 'tp'), may hold values from -6 to 6
- piece_owner: int32 [192, 2], P('req'), may hold values from -1 to 63, as said below
- cache_len: int32 [64], replicated, may hold values from 1 to 1016, as said below
- out_weight: bfloat16 [4096, 4096], P('tp', 'req'), may hold values from -0.09375 to 0.09375
Outputs:
- mixed: bfloat16 [64, 28, 4096], P('tp', None, 'req')
- cache_out: bfloat16 [192, 256, 2048], P('req', None, 'tp')
Inputs may be any that keep to these rules, and one draw needn't show every extreme that they name: tree_parent[r, 0] = -1 and 0 <= tree_parent[r, i] < i for i >= 1; tokens 1 to 7 have parent i - 1. accepted_path[r] lists, root first, the tokens on the path from token 0 to some token of request r's tree, then -1 entries; it holds 1 to 8 tokens, and 8 for some request. piece_owner[s] = (r, p) means slot s holds cache rows p * 256 to p * 256 + 255 of request r; (-1, -1) marks an unused slot. For each request r the pieces 0 to (cache_len[r] + 7) // 256 stand in exactly one slot each, and no other pieces do. cache_len[r] + 8 <= 1024.
All inputs are finite; a program needn't handle non-finite values.
Results may differ from a plain program's by a relative error of at most 0.02.
Values may be sent and summed in bfloat16 or wider, within the bound.
No kernel may reach another device: no remote copies, remote signals or barrier semaphores. Data moves between devices by JAX's collectives and lax.ppermute only.
A program may use at most 64 MiB of HBM per device.

v0:
```python
import math
import jax
import jax.numpy as jnp
from jax import lax
from jax.sharding import PartitionSpec as P

HD = 128
NEG = -1e30


def ancestors(parent):
    tree_size = parent.shape[-1]
    node_ids = lax.broadcasted_iota(jnp.int32, (tree_size, tree_size), 1)
    parent_hot = (parent[..., :, None] == node_ids).astype(jnp.float32)
    reached = jnp.minimum(parent_hot + jnp.eye(tree_size, dtype=jnp.float32), 1.0)
    for rounds in range(max(1, (tree_size - 1).bit_length())):
        reached = jnp.minimum(
            jnp.einsum("rij,rjk->rik", reached, reached, precision=lax.Precision.HIGHEST), 1.0
        )
    return reached


def shards(
    queries, tree_kv, tree_parent, accepted_path, cache_kv, piece_owner, cache_len, out_weight
):
    kvheads_local = tree_kv.shape[-1] // (2 * HD)
    heads_local = queries.shape[-1] // HD
    group_size = heads_local // kvheads_local
    tree_size = queries.shape[1]
    slot_count = cache_kv.shape[0]
    piece_rows = cache_kv.shape[1]
    depth_most = accepted_path.shape[1]
    scaling = 1.0 / math.sqrt(HD)
    every_query = lax.all_gather(queries, "req", axis=0, tiled=True)
    req_total = every_query.shape[0]
    owner_req = piece_owner[:, 0]
    owner_piece = piece_owner[:, 1]
    safe_req = jnp.maximum(owner_req, 0)
    slot_query = every_query[safe_req].reshape(slot_count, tree_size, kvheads_local, group_size, HD)
    stored = cache_kv.reshape(slot_count, piece_rows, kvheads_local, 2, HD)
    row_pos = owner_piece[:, None] * piece_rows + lax.broadcasted_iota(
        jnp.int32, (slot_count, piece_rows), 1
    )
    visible = (owner_req >= 0)[:, None] & (row_pos < cache_len[safe_req][:, None])
    wide_mask = visible[:, None, None, None, :]
    scores = (
        jnp.einsum(
            "stkgd,spkd->stkgp", slot_query, stored[:, :, :, 0], preferred_element_type=jnp.float32
        )
        * scaling
    )
    scores = jnp.where(wide_mask, scores, NEG)
    slot_peak = jnp.max(scores, -1)
    expo = jnp.where(wide_mask, jnp.exp(scores - slot_peak[..., None]), 0.0)
    slot_den = jnp.sum(expo, -1)
    weights = expo.astype(jnp.bfloat16)
    slot_num = jnp.einsum(
        "stkgp,spkd->stkgd", weights, stored[:, :, :, 1], preferred_element_type=jnp.float32
    )
    request_ids = lax.broadcasted_iota(jnp.int32, (req_total, slot_count), 0)
    member = (owner_req[None, :] == request_ids)[:, :, None, None, None]
    req_peak = jnp.max(jnp.where(member, slot_peak[None], NEG), axis=1)
    factor = jnp.where(
        member, jnp.exp(jnp.where(member, slot_peak[None] - req_peak[:, None], 0.0)), 0.0
    )
    req_den = jnp.sum(factor * slot_den[None], axis=1)
    req_num = jnp.einsum("rstkg,stkgd->rtkgd", factor, slot_num, precision=lax.Precision.HIGHEST)
    peak_table = req_peak.reshape(req_total, tree_size, heads_local)
    den_table = req_den.reshape(req_total, tree_size, heads_local)
    num_table = req_num.reshape(req_total, tree_size, heads_local * HD)
    own_index = lax.axis_index("req")
    got_peak, got_den, got_num = (
        lax.all_to_all(
            peak_table.astype(jnp.bfloat16), "req", split_axis=0, concat_axis=0, tiled=True
        ).astype(peak_table.dtype),
        lax.all_to_all(
            den_table.astype(jnp.bfloat16), "req", split_axis=0, concat_axis=0, tiled=True
        ).astype(den_table.dtype),
        lax.all_to_all(
            num_table.astype(jnp.bfloat16), "req", split_axis=0, concat_axis=0, tiled=True
        ).astype(num_table.dtype),
    )
    cache_peak = jnp.max(got_peak, axis=0)
    source_scale = jnp.exp(got_peak - cache_peak[None])
    cache_den = jnp.sum(source_scale * got_den, axis=0)
    got_rows = got_num.reshape(got_num.shape[0], tree_size, heads_local, HD)
    cache_num = jnp.sum(source_scale[..., None] * got_rows, axis=0)
    reached = ancestors(tree_parent)[0]
    home_query = queries[0].reshape(tree_size, kvheads_local, group_size, HD)
    fresh = tree_kv[0].reshape(tree_size, kvheads_local, 2, HD)
    tree_mask = reached[:, None, None, :] > 0.5
    tree_scores = (
        jnp.einsum("ikgd,jkd->ikgj", home_query, fresh[:, :, 0], preferred_element_type=jnp.float32)
        * scaling
    )
    tree_scores = jnp.where(tree_mask, tree_scores, NEG)
    tree_peak = jnp.max(tree_scores, -1)
    tree_exp = jnp.where(tree_mask, jnp.exp(tree_scores - tree_peak[..., None]), 0.0)
    tree_den = jnp.sum(tree_exp, -1).reshape(tree_size, heads_local)
    tree_num = jnp.einsum(
        "ikgj,jkd->ikgd",
        tree_exp.astype(jnp.bfloat16),
        fresh[:, :, 1],
        preferred_element_type=jnp.float32,
    )
    tree_num = tree_num.reshape(tree_size, heads_local, HD)
    tree_peak = tree_peak.reshape(tree_size, heads_local)
    total_peak = jnp.maximum(cache_peak, tree_peak)
    cache_scale = jnp.exp(cache_peak - total_peak)
    tree_scale = jnp.exp(tree_peak - total_peak)
    denom = cache_den * cache_scale + tree_den * tree_scale
    numer = cache_num * cache_scale[..., None] + tree_num * tree_scale[..., None]
    attention = (
        (numer / denom[..., None]).reshape(1, tree_size, heads_local * HD).astype(jnp.bfloat16)
    )
    piece = lax.all_gather(attention, "req", axis=0, tiled=True)
    flat_rows = piece.reshape(piece.shape[0] * piece.shape[1], piece.shape[2])
    product = jnp.dot(flat_rows, out_weight, preferred_element_type=jnp.float32)
    terms = product.reshape(piece.shape[0], piece.shape[1], out_weight.shape[1])
    mixed = lax.psum_scatter(terms.astype(jnp.bfloat16), "tp", scatter_dimension=0, tiled=True)
    own_path = lax.dynamic_index_in_dim(accepted_path, own_index, 0, keepdims=False)
    picked = tree_kv[0][jnp.maximum(own_path, 0)]
    picked = jnp.where((own_path >= 0)[:, None], picked, jnp.zeros_like(picked))
    all_rows = lax.all_gather(picked[None], "req", axis=0, tiled=True)
    counts = jnp.sum((accepted_path >= 0).astype(jnp.int32), axis=1)
    offset = row_pos - cache_len[safe_req][:, None]
    writing = (owner_req >= 0)[:, None] & (offset >= 0) & (offset < counts[safe_req][:, None])
    slot_rows = all_rows[safe_req]
    chosen = jnp.take_along_axis(slot_rows, jnp.clip(offset, 0, depth_most - 1)[:, :, None], axis=1)
    cache_out = jnp.where(writing[:, :, None], chosen, cache_kv)
    return (mixed, cache_out)


def solution(mesh):
    return jax.shard_map(
        shards,
        mesh=mesh,
        in_specs=(
            P("req", None, "tp"),
            P("req", None, "tp"),
            P("req", None),
            P(),
            P("req", None, "tp"),
            P("req", None),
            P(),
            P("tp", "req"),
        ),
        out_specs=(P("tp", None, "req"), P("req", None, "tp")),
        check_vma=False,
    )
```

profile of v0, /device:TPU:2, one launch (start us, length us, event | category | flops | bytes accessed | tf_op | source)
XLA Modules:
  0.0 331.0 jit_solution(16705288890588195445)
XLA Ops:
  7.2 0.7 all-gather.3.cloned.1.call-update
  7.9 1.2 copy.126
  9.1 0.8 slice_bitcast_fusion.4
  9.9 0.7 convert_reduce_fusion
  10.6 0.6 gather_fusion.2
  11.2 1.3 gather_fusion
  12.6 0.7 compare_bitcast_fusion
  13.3 84.3 %all-gather.3.cloned.1.call-done = bf16[64,28,512]{2,1,0:T(8,128)(2,1)} async-done(((bf16[1,28,512]{2,1,0:T(8,128)(2,1)}), bf16[64,28,512]{2,1,0:T(8,128)(2,1)}) %all-gather.3.cloned.1.call-update) | async-done | bytes 1835024 | tf_op jit(solution)/shard_map/all_gather | solution.py:34
  97.6 2.1 gather_fusion.1
  99.8 0.3 fusion.62
  100.1 0.1 copy.129
  100.2 0.2 fusion.11
  100.5 0.3 fusion.19
  100.7 0.2 select_reduce_fusion
  100.9 0.8 copy.130
  101.7 8.0 %all-to-all-start = ((bf16[64,28,4]{1,2,0:T(4,128)(2,1)}), bf16[64,28,4]{1,2,0:T(4,128)(2,1)S(1)}, u32[]{:S(2)}, u32[]{:S(2)}) async-start(bf16[64,28,4]{1,2,0:T(4,128)(2,1)} %copy.130), calls=%async_computation | async-start | bytes 131072 | tf_op jit(solution)/shard_map/all_to_all | solution.py:73
  109.7 0.1 copy.150
  109.8 0.3 multiply_reduce_fusion.1
  110.1 0.1 copy.137
  110.2 0.8 copy.151
  110.9 7.5 %all-to-all-done = bf16[64,28,4]{1,2,0:T(4,128)(2,1)S(1)} async-done(((bf16[64,28,4]{1,2,0:T(4,128)(2,1)}), bf16[64,28,4]{1,2,0:T(4,128)(2,1)S(1)}, u32[]{:S(2)}, u32[]{:S(2)}) %all-to-all-start) | async-done | bytes 14368 | tf_op jit(solution)/shard_map/all_to_all | solution.py:73
  118.5 5.5 %all-to-all-start.2 = ((bf16[64,28,4]{1,2,0:T(4,128)(2,1)}), bf16[64,28,4]{1,2,0:T(4,128)(2,1)S(1)}, u32[]{:S(2)}, u32[]{:S(2)}) async-start(bf16[64,28,4]{1,2,0:T(4,128)(2,1)} %copy.151), calls=%async_computation.2 | async-start | bytes 131072 | tf_op jit(solution)/shard_map/all_to_all | solution.py:76
  124.0 6.0 %convert_bitcast_fusion = bf16[64,28,1,4,128]{4,0,3,1,2:T(8,128)(2,1)S(1)} fusion(f32[3,28,4,128]{3,1,2,0:T(8,128)S(1)} %fusion.19, f32[64,28,4]{0,2,1:T(4,128)S(1)} %select_reduce_fusion, f32[3,28,4]{0,2,1:T(4,128)S(1)} %copy.137, pred[64,3]{0,1:T(4,128)(4,1)S(1)} %iota_compare_fusion), kind=kOutput, calls=%fused_computation.9 | convolution fusion | flops 34012160 | bytes 2037248 | tf_op jit(solution)/shard_map/rstkg,stkgd->rtkgd/dot_general | solution.py:67
  130.0 1.4 copy.161
  131.4 1.8 reshape.676
  133.3 10.7 %all-to-all-start.1 = ((bf16[64,28,512]{2,1,0:T(8,128)(2,1)}), bf16[64,28,512]{2,1,0:T(8,128)(2,1)S(1)}, u32[]{:S(2)}, u32[]{:S(2)}) async-start(bf16[64,28,512]{2,1,0:T(8,128)(2,1)} %reshape.676), calls=%async_computation.1 | async-start | bytes 4194304 | tf_op jit(solution)/shard_map/all_to_all | solution.py:79
  144.1 0.1 fusion.42
  144.2 0.1 convolution_minimum_fusion.4
  144.3 0.1 convolution_minimum_fusion.3
  144.5 0.1 convolution_minimum_fusion.2
  144.6 0.1 convolution_minimum_fusion.1
  144.8 0.2 fusion.10
  144.9 0.1 copy.142
  145.1 0.2 fusion.61
  145.3 0.2 convolution_bitcast_fusion
  145.6 0.1 copy.134
  145.7 0.1 copy.131
  145.9 0.1 copy.152
  146.0 0.2 subtract_exponential_fusion
  146.3 0.1 copy.155
  146.4 0.1 copy.149
  146.5 0.1 copy.145
  146.6 0.4 copy.135
  147.0 3.5 %mul.113 = f32[64,28,4,128]{3,2,0,1:T(4,128)} broadcast(f32[64,28,4]{2,0,1:T(8,128)S(1)} %copy.135), dimensions={0,1,2} | broadcast | bytes 3698688 | tf_op jit(solution)/shard_map/mul | solution.py:87
  150.5 5.2 %mul.114 = f32[64,28,512]{2,0,1:T(8,128)} reshape(f32[64,28,4,128]{3,2,0,1:T(4,128)} %mul.113) | data formatting | bytes 7340032 | tf_op jit(solution)/shard_map/mul | solution.py:87
  155.7 37.8 %all-to-all-done.1 = bf16[64,28,512]{2,1,0:T(8,128)(2,1)S(1)} async-done(((bf16[64,28,512]{2,1,0:T(8,128)(2,1)}), bf16[64,28,512]{2,1,0:T(8,128)(2,1)S(1)}, u32[]{:S(2)}, u32[]{:S(2)}) %all-to-all-start.1) | async-done | bytes 1835040 | tf_op jit(solution)/shard_map/all_to_all | solution.py:79
  193.5 3.6 %multiply_reduce_fusion = f32[28,512]{1,0:T(8,128)S(1)} fusion(f32[64,28,512]{2,0,1:T(8,128)} %mul.114, bf16[64,28,512]{2,1,0:T(8,128)(2,1)S(1)} %all-to-all-done.1), kind=kLoop, calls=%fused_computation.6 | loop fusion | flops 2738176 | bytes 5562368 | tf_op jit(solution)/shard_map/reduce_sum | solution.py:87
  197.2 0.1 mul.123
  197.3 0.1 fusion.30
  197.5 0.6 copy.156
  198.2 0.2 maximum_reduce_fusion
  198.4 0.6 gather_fusion.3
  199.0 0.2 compare_reduce_fusion
  199.2 37.4 %all_gather.11 = bf16[64,8,256]{2,1,0:T(8,128)(2,1)S(1)} all-gather(bf16[1,8,256]{2,1,0:T(8,128)(2,1)S(1)} %bitcast_select_fusion), channel_id=1, replica_groups=mesh['req'=64,'tp'=8] {'req'}, dimensions={0}, use_global_device_ids=true | all-gather | bytes 266240 | tf_op jit(solution)/shard_map/all_gather | solution.py:124
  236.7 0.5 gather_fusion.4
  237.2 41.2 %all-gather.5.cloned.1.call-done = bf16[64,28,512]{2,1,0:T(8,128)(2,1)} async-done(((bf16[1,28,512]{2,1,0:T(8,128)(2,1)}), bf16[64,28,512]{2,1,0:T(8,128)(2,1)}) %all-gather.5.cloned.1.call-update) | async-done | bytes 1835024 | tf_op jit(solution)/shard_map/all_gather | solution.py:116
  278.4 3.7 %fusion.2 = bf16[64,28,64]{2,0,1:T(8,128)(2,1)S(1)} fusion(bf16[64,28,512]{2,1,0:T(8,128)(2,1)} %all-gather.5.cloned.1.call-done, bf16[512,64]{0,1:T(8,128)(2,1)S(1)} %copy-done), kind=kOutput, calls=%fused_computation.10 | convolution fusion | flops 117555200 | bytes 2129920 | tf_op jit(solution)/shard_map/dot_general | solution.py:118
  282.1 0.3 copy.162
  282.4 1.1 reshape.677
  283.7 4.2 %gather_fusion.5 = bf16[768,256]{1,0:T(8,128)(2,1)S(1)} fusion(bf16[3,8,256]{2,1,0:T(8,128)(2,1)S(1)} %gather_fusion.4, s32[768]{0:T(1024)S(1)} %reshape.664), kind=kCustom, calls=%fused_computation.5 | custom fusion | bytes 792576 | tf_op jit(solution)/shard_map/jit(take_along_axis)/gather | solution.py:129
  287.9 1.0 select_select_fusion
  288.9 34.0 %reduce-scatter.4.cloned.1.call-done = bf16[8,1792]{1,0:T(8,128)(2,1)} async-done(((bf16[64,1792]{1,0:T(8,128)(2,1)}), bf16[8,1792]{1,0:T(8,128)(2,1)}) %reduce-scatter.4.cloned.1.call-update) | async-done | bytes 28688
  322.9 0.9 reshape.678
  323.8 0.6 copy.163
  (37 shorter events, 1.1 us)
Async XLA Ops:
  7.2 271.3 %copy-start = (bf16[512,64]{0,1:T(8,128)(2,1)S(1)}, bf16[512,64]{0,1:T(8,128)(2,1)}, u32[]{:S(2)}) copy-start(bf16[512,64]{0,1:T(8,128)(2,1)} %param.15) | copy-start | bytes 196612
  7.2 90.4 %all-gather.3.cloned.1.call-start = ((), (), s32[]{:S(2)}) async-start(), calls=%async_computation.4 | async-start | bytes 2129920 | tf_op jit(solution)/shard_map/all_gather | solution.py:34
  101.7 16.8 %all-to-all-start = ((bf16[64,28,4]{1,2,0:T(4,128)(2,1)}), bf16[64,28,4]{1,2,0:T(4,128)(2,1)S(1)}, u32[]{:S(2)}, u32[]{:S(2)}) async-start(bf16[64,28,4]{1,2,0:T(4,128)(2,1)} %copy.130), calls=%async_computation | async-start | bytes 131072 | tf_op jit(solution)/shard_map/all_to_all | solution.py:73
  118.5 14.8 %all-to-all-start.2 = ((bf16[64,28,4]{1,2,0:T(4,128)(2,1)}), bf16[64,28,4]{1,2,0:T(4,128)(2,1)S(1)}, u32[]{:S(2)}, u32[]{:S(2)}) async-start(bf16[64,28,4]{1,2,0:T(4,128)(2,1)} %copy.151), calls=%async_computation.2 | async-start | bytes 131072 | tf_op jit(solution)/shard_map/all_to_all | solution.py:76
  133.3 10.7 %copy-start.3 = (bf16[1,28,512]{2,1,0:T(8,128)(2,1)S(1)}, bf16[1,28,512]{2,1,0:T(8,128)(2,1)}, u32[]{:S(2)}) copy-start(bf16[1,28,512]{2,1,0:T(8,128)(2,1)} %param.8) | copy-start | bytes 86020
  133.3 10.8 %copy-start.2 = (bf16[1,28,256]{2,1,0:T(8,128)(2,1)S(1)}, bf16[1,28,256]{2,1,0:T(8,128)(2,1)}, u32[]{:S(2)}) copy-start(bf16[1,28,256]{2,1,0:T(8,128)(2,1)} %param.9) | copy-start | bytes 43012
  133.3 10.8 %copy-start.5 = (s32[1,28]{1,0:T(1,128)S(1)}, s32[1,28]{1,0:T(1,128)}, u32[]{:S(2)}) copy-start(s32[1,28]{1,0:T(1,128)} %param.10) | copy-start | bytes 340
  133.3 60.2 %all-to-all-start.1 = ((bf16[64,28,512]{2,1,0:T(8,128)(2,1)}), bf16[64,28,512]{2,1,0:T(8,128)(2,1)S(1)}, u32[]{:S(2)}, u32[]{:S(2)}) async-start(bf16[64,28,512]{2,1,0:T(8,128)(2,1)} %reshape.676), calls=%async_computation.1 | async-start | bytes 4194304 | tf_op jit(solution)/shard_map/all_to_all | solution.py:79
  143.9 134.5 %all-gather.5.cloned.1.call-start = ((), (), s32[]{:S(2)}) async-start(), calls=%async_computation.5 | async-start | bytes 2129920 | tf_op jit(solution)/shard_map/all_gather | solution.py:116
  155.7 42.5 %copy-start.4 = (s32[64,8]{0,1:T(8,128)S(1)}, s32[64,8]{0,1:T(8,128)}, u32[]{:S(2)}) copy-start(s32[64,8]{0,1:T(8,128)} %param.11) | copy-start | bytes 6148
  198.1 124.8 %reduce-scatter.4.cloned.1.call-start = ((), (), s32[]{:S(2)}) async-start(), calls=%async_computation.6 | async-start | bytes 258048
  283.6 4.3 %copy-start.1 = (bf16[3,256,256]{2,1,0:T(8,128)(2,1)S(1)}, bf16[3,256,256]{2,1,0:T(8,128)(2,1)}, u32[]{:S(2)}) copy-start(bf16[3,256,256]{2,1,0:T(8,128)(2,1)} %param.12) | copy-start | bytes 1179652
Sparse Core Ops, SparseCore 0:
  11.4 86.1 all-gather.2
  198.3 80.1 all-gather.4
  283.7 39.1 reduce-scatter.3
where the time goes:
time: 332 us; the launch traced here: 331 us
  waiting for transfers between devices  206 us (62%)
  blocking collectives  37.4 us (11%)
  local copies, waits for them, and re-layouts  29.6 us (9%)
  starting transfers between devices  24.3 us (7%)
  between operations  14.1 us (4%)
  matrix products  11.4 us (3%)
  other arithmetic  8.73 us (3%)
    all_gather x1, waiting for transfers between devices, shards(): every_query = lax.all_gather(queries, 'req', axis=0, tiled=True)  84.3 us
    all_gather x1, waiting for transfers between devices, shards(): piece = lax.all_gather(attention, 'req', axis=0, tiled=True)  41.2 us
    all_to_all x1, waiting for transfers between devices, shards(): lax.all_to_all(num_table.astype(jnp.bfloat16), 'req', split_axis=0, conca...  37.8 us
    all_gather x1, blocking collectives, shards(): all_rows = lax.all_gather(picked[None], 'req', axis=0, tiled=True)  37.4 us
    unnamed x4, waiting for transfers between devices  34.7 us
    all_to_all x1, starting transfers between devices, shards(): lax.all_to_all(num_table.astype(jnp.bfloat16), 'req', split_axis=0, conca...  10.7 us
    mul x2, local copies, waits for them, and re-layouts, shards(): cache_num = jnp.sum(source_scale[..., None] * got_rows, axis=0)  8.76 us
    all_to_all x1, starting transfers between devices, shards(): lax.all_to_all(peak_table.astype(jnp.bfloat16), 'req', split_axis=0, conc...  7.97 us
  transfers between devices with their start and end apart: 6, of which 5 were waited for; matrix products, arithmetic and copies ran while one was open for 10% of the time, Pallas kernels for 0%

commit v1 on v0

--- a/solution.py
+++ b/solution.py
@@ -6,6 +6,14 @@
 
 HD = 128
 NEG = -1e30
+
+
+def gather_from_all(array, axis, dim):
+    size = lax.axis_size(axis)
+    repeats = [size if d == dim else 1 for d in range(array.ndim)]
+    return lax.all_to_all(
+        jnp.tile(array, repeats), axis, split_axis=dim, concat_axis=dim, tiled=True
+    )
 
 
 def ancestors(parent):
@@ -31,7 +39,7 @@
     piece_rows = cache_kv.shape[1]
     depth_most = accepted_path.shape[1]
     scaling = 1.0 / math.sqrt(HD)
-    every_query = lax.all_gather(queries, "req", axis=0, tiled=True)
+    every_query = gather_from_all(queries, "req", 0)
     req_total = every_query.shape[0]
     owner_req = piece_owner[:, 0]
     owner_piece = piece_owner[:, 1]

time: 332 us -> 305 us (0.919)
  waiting for transfers between devices: 206 us -> 167 us
  starting transfers between devices: 24.3 us -> 34.6 us
    all_gather x1 -> x0, waiting for transfers between devices: 84.3 us -> none  [shards(): every_query = lax.all_gather(queries, 'req', axis=0, tiled=True)]
    all_to_all x0 -> x1, waiting for transfers between devices: none -> 47.2 us  [gather_from_all(): lax.all_to_all(jnp.tile(array, repeats), axis, split_axis=dim, concat_axi...]
    all_to_all x0 -> x1, starting transfers between devices: none -> 10.8 us  [gather_from_all(): lax.all_to_all(jnp.tile(array, repeats), axis, split_axis=dim, concat_axi...]
    all_to_all x1, waiting for transfers between devices: 37.8 us -> 34.4 us  [shards(): lax.all_to_all(num_table.astype(jnp.bfloat16), 'req', split_axis=0, conca...]
    unnamed x4 -> x3, waiting for transfers between devices: 34.7 us -> 34 us
  transfers between devices with their start and end apart: 6 -> 6, of which waited for: 5 -> 5; matrix products, arithmetic and copies ran while one was open for 10% -> 11% of each run, Pallas kernels for 0% -> 0%
where the time goes in v1:
time: 305 us; the launch traced here: 304 us
  waiting for transfers between devices  167 us (55%)
  blocking collectives  37.4 us (12%)
  starting transfers between devices  34.6 us (11%)
  local copies, waits for them, and re-layouts  31.4 us (10%)
  between operations  14.5 us (5%)
  matrix products  11.3 us (4%)
  other arithmetic  7.49 us (2%)
    all_to_all x1, waiting for transfers between devices, gather_from_all(): lax.all_to_all(jnp.tile(array, repeats), axis, split_axis=dim, concat_axi...  47.2 us
    all_gather x1, waiting for transfers between devices, shards(): piece = lax.all_gather(attention, 'req', axis=0, tiled=True)  44.1 us
    all_gather x1, blocking collectives, shards(): all_rows = lax.all_gather(picked[None], 'req', axis=0, tiled=True)  37.4 us
    all_to_all x1, waiting for transfers between devices, shards(): lax.all_to_all(num_table.astype(jnp.bfloat16), 'req', split_axis=0, conca...  34.4 us
    unnamed x3, waiting for transfers between devices  34 us
    all_to_all x1, starting transfers between devices, gather_from_all(): lax.all_to_all(jnp.tile(array, repeats), axis, split_axis=dim, concat_axi...  10.8 us
    all_to_all x1, starting transfers between devices, shards(): lax.all_to_all(num_table.astype(jnp.bfloat16), 'req', split_axis=0, conca...  10.5 us
    mul x2, local copies, waits for them, and re-layouts, shards(): cache_num = jnp.sum(source_scale[..., None] * got_rows, axis=0)  8.76 us
  transfers between devices with their start and end apart: 6, of which 5 were waited for; matrix products, arithmetic and copies ran while one was open for 11% of the time, Pallas kernels for 0%

profile of v1, /device:TPU:2, one launch (start us, length us, event | category | flops | bytes accessed | tf_op | source)
XLA Modules:
  0.0 304.1 jit_solution(15334267616857455319)
XLA Ops:
  7.2 2.4 tile.10
  9.6 10.8 %all-to-all-start = ((bf16[64,28,512]{2,1,0:T(8,128)(2,1)}), bf16[64,28,512]{2,1,0:T(8,128)(2,1)S(1)}, u32[]{:S(2)}, u32[]{:S(2)}) async-start(bf16[64,28,512]{2,1,0:T(8,128)(2,1)} %tile.10), calls=%async_computation | async-start | bytes 4194304 | tf_op jit(solution)/shard_map/all_to_all | solution.py:14
  20.4 0.2 copy.125
  20.7 0.6 gather_fusion.2
  21.3 0.6 gather_fusion
  22.0 0.7 fusion.50
  22.7 47.2 %all-to-all-done = bf16[64,28,512]{2,1,0:T(8,128)(2,1)S(1)} async-done(((bf16[64,28,512]{2,1,0:T(8,128)(2,1)}), bf16[64,28,512]{2,1,0:T(8,128)(2,1)S(1)}, u32[]{:S(2)}, u32[]{:S(2)}) %all-to-all-start) | async-done | bytes 1835040 | tf_op jit(solution)/shard_map/all_to_all | solution.py:14
  69.9 0.6 gather_fusion.1
  70.5 0.3 fusion.62
  70.8 0.1 copy.128
  70.9 0.2 fusion.11
  71.2 0.2 fusion.19
  71.4 0.2 select_reduce_fusion
  71.7 0.8 copy.129
  72.4 7.5 %all-to-all-start.1 = ((bf16[64,28,4]{1,2,0:T(4,128)(2,1)}), bf16[64,28,4]{1,2,0:T(4,128)(2,1)S(1)}, u32[]{:S(2)}, u32[]{:S(2)}) async-start(bf16[64,28,4]{1,2,0:T(4,128)(2,1)} %copy.129), calls=%async_computation.1 | async-start | bytes 131072 | tf_op jit(solution)/shard_map/all_to_all | solution.py:81
  79.9 0.1 copy.149
  80.1 0.3 multiply_reduce_fusion.1
  80.4 0.1 copy.136
  80.5 0.8 copy.150
  81.2 7.5 %all-to-all-done.1 = bf16[64,28,4]{1,2,0:T(4,128)(2,1)S(1)} async-done(((bf16[64,28,4]{1,2,0:T(4,128)(2,1)}), bf16[64,28,4]{1,2,0:T(4,128)(2,1)S(1)}, u32[]{:S(2)}, u32[]{:S(2)}) %all-to-all-start.1) | async-done | bytes 14368 | tf_op jit(solution)/shard_map/all_to_all | solution.py:81
  88.8 5.5 %all-to-all-start.3 = ((bf16[64,28,4]{1,2,0:T(4,128)(2,1)}), bf16[64,28,4]{1,2,0:T(4,128)(2,1)S(1)}, u32[]{:S(2)}, u32[]{:S(2)}) async-start(bf16[64,28,4]{1,2,0:T(4,128)(2,1)} %copy.150), calls=%async_computation.3 | async-start | bytes 131072 | tf_op jit(solution)/shard_map/all_to_all | solution.py:84
  94.3 6.0 %convert_bitcast_fusion = bf16[64,28,1,4,128]{4,0,3,1,2:T(8,128)(2,1)S(1)} fusion(f32[3,28,4,128]{3,1,2,0:T(8,128)S(1)} %fusion.19, f32[64,28,4]{0,2,1:T(4,128)S(1)} %select_reduce_fusion, f32[3,28,4]{0,2,1:T(4,128)S(1)} %copy.136, pred[64,3]{0,1:T(4,128)(4,1)S(1)} %iota_compare_fusion), kind=kOutput, calls=%fused_computation.9 | convolution fusion | flops 34012160 | bytes 2037248 | tf_op jit(solution)/shard_map/rstkg,stkgd->rtkgd/dot_general | solution.py:75
  100.3 1.4 copy.160
  101.7 1.8 reshape.679
  103.6 10.5 %all-to-all-start.2 = ((bf16[64,28,512]{2,1,0:T(8,128)(2,1)}), bf16[64,28,512]{2,1,0:T(8,128)(2,1)S(1)}, u32[]{:S(2)}, u32[]{:S(2)}) async-start(bf16[64,28,512]{2,1,0:T(8,128)(2,1)} %reshape.679), calls=%async_computation.2 | async-start | bytes 4194304 | tf_op jit(solution)/shard_map/all_to_all | solution.py:87
  114.1 0.3 all-gather.2.cloned.1.call-start
  114.4 0.1 fusion.42
  114.5 0.1 convolution_minimum_fusion.4
  114.6 0.1 convolution_minimum_fusion.3
  114.8 0.1 convolution_minimum_fusion.2
  115.0 0.1 convolution_minimum_fusion.1
  115.1 0.2 fusion.10
  115.3 0.1 copy.141
  115.4 0.2 fusion.61
  115.6 0.2 convolution_bitcast_fusion
  116.0 0.1 copy.133
  116.1 0.1 copy.130
  116.2 0.1 copy.151
  116.3 0.7 subtract_exponential_fusion
  117.1 0.1 copy.153
  117.2 0.7 copy.154
  117.9 0.7 copy.148
  118.6 0.7 copy.144
  119.2 1.2 copy.134
  120.4 3.5 %mul.113 = f32[64,28,4,128]{3,2,0,1:T(4,128)} broadcast(f32[64,28,4]{2,0,1:T(8,128)S(1)} %copy.134), dimensions={0,1,2} | broadcast | bytes 3698688 | tf_op jit(solution)/shard_map/mul | solution.py:95
  124.0 5.2 %mul.114 = f32[64,28,512]{2,0,1:T(8,128)} reshape(f32[64,28,4,128]{3,2,0,1:T(4,128)} %mul.113) | data formatting | bytes 7340032 | tf_op jit(solution)/shard_map/mul | solution.py:95
  129.2 34.4 %all-to-all-done.2 = bf16[64,28,512]{2,1,0:T(8,128)(2,1)S(1)} async-done(((bf16[64,28,512]{2,1,0:T(8,128)(2,1)}), bf16[64,28,512]{2,1,0:T(8,128)(2,1)S(1)}, u32[]{:S(2)}, u32[]{:S(2)}) %all-to-all-start.2) | async-done | bytes 1835040 | tf_op jit(solution)/shard_map/all_to_all | solution.py:87
  163.6 3.3 %multiply_reduce_fusion = f32[28,512]{1,0:T(8,128)S(1)} fusion(f32[64,28,512]{2,0,1:T(8,128)} %mul.114, bf16[64,28,512]{2,1,0:T(8,128)(2,1)S(1)} %all-to-all-done.2), kind=kLoop, calls=%fused_computation.6 | loop fusion | flops 2738176 | bytes 5562368 | tf_op jit(solution)/shard_map/reduce_sum | solution.py:95
  167.2 0.1 fusion.30
  167.4 0.6 copy.155
  168.1 0.2 maximum_reduce_fusion
  168.3 0.6 gather_fusion.3
  168.8 0.2 compare_reduce_fusion
  169.1 37.4 %all_gather.7 = bf16[64,8,256]{2,1,0:T(8,128)(2,1)S(1)} all-gather(bf16[1,8,256]{2,1,0:T(8,128)(2,1)S(1)} %bitcast_select_fusion), channel_id=1, replica_groups=mesh['req'=64,'tp'=8] {'req'}, dimensions={0}, use_global_device_ids=true | all-gather | bytes 266240 | tf_op jit(solution)/shard_map/all_gather | solution.py:132
  206.6 0.5 gather_fusion.4
  207.1 44.1 %all-gather.2.cloned.1.call-done = bf16[64,28,512]{2,1,0:T(8,128)(2,1)} async-done(((bf16[1,28,512]{2,1,0:T(8,128)(2,1)}), bf16[64,28,512]{2,1,0:T(8,128)(2,1)}) %all-gather.2.cloned.1.call-update) | async-done | bytes 1835024 | tf_op jit(solution)/shard_map/all_gather | solution.py:124
  251.2 3.7 %fusion.2 = bf16[64,28,64]{2,0,1:T(8,128)(2,1)S(1)} fusion(bf16[64,28,512]{2,1,0:T(8,128)(2,1)} %all-gather.2.cloned.1.call-done, bf16[512,64]{0,1:T(8,128)(2,1)S(1)} %copy-done), kind=kOutput, calls=%fused_computation.10 | convolution fusion | flops 117555200 | bytes 2129920 | tf_op jit(solution)/shard_map/dot_general | solution.py:126
  254.9 0.3 copy.161
  255.3 1.1 reshape.680
  256.5 4.2 %gather_fusion.5 = bf16[768,256]{1,0:T(8,128)(2,1)S(1)} fusion(bf16[3,8,256]{2,1,0:T(8,128)(2,1)S(1)} %gather_fusion.4, s32[768]{0:T(1024)S(1)} %reshape.667), kind=kCustom, calls=%fused_computation.5 | custom fusion | bytes 792576 | tf_op jit(solution)/shard_map/jit(take_along_axis)/gather | solution.py:137
  260.7 1.0 select_select_fusion
  261.8 34.0 %reduce-scatter.4.cloned.1.call-done = bf16[8,1792]{1,0:T(8,128)(2,1)} async-done(((bf16[64,1792]{1,0:T(8,128)(2,1)}), bf16[8,1792]{1,0:T(8,128)(2,1)}) %reduce-scatter.4.cloned.1.call-update) | async-done | bytes 28688
  295.7 0.9 reshape.681
  296.6 0.6 copy.162
  (59 shorter events, 1.0 us)
Async XLA Ops:
  7.2 244.1 %copy-start = (bf16[512,64]{0,1:T(8,128)(2,1)S(1)}, bf16[512,64]{0,1:T(8,128)(2,1)}, u32[]{:S(2)}) copy-start(bf16[512,64]{0,1:T(8,128)(2,1)} %param.15) | copy-start | bytes 196612
  9.6 10.8 %copy-start.2 = (bf16[3,256,256]{2,1,0:T(8,128)(2,1)S(1)}, bf16[3,256,256]{2,1,0:T(8,128)(2,1)}, u32[]{:S(2)}) copy-start(bf16[3,256,256]{2,1,0:T(8,128)(2,1)} %param.12) | copy-start | bytes 1179652
  9.6 11.0 %copy-start.15 = (s32[3,2]{0,1:T(2,128)S(1)}, s32[3,2]{0,1:T(2,128)}, u32[]{:S(2)}) copy-start(s32[3,2]{0,1:T(2,128)} %param.13) | copy-start | bytes 76
  9.6 11.1 %copy-start.8 = (s32[64,8]{0,1:T(8,128)S(1)}, s32[64,8]{0,1:T(8,128)}, u32[]{:S(2)}) copy-start(s32[64,8]{0,1:T(8,128)} %param.11) | copy-start | bytes 6148
  9.6 11.7 %copy-start.1 = (s32[64]{0:T(128)S(1)}, s32[64]{0:T(128)}, u32[]{:S(2)}) copy-start(s32[64]{0:T(128)} %param.14) | copy-start | bytes 772
  9.6 60.3 %all-to-all-start = ((bf16[64,28,512]{2,1,0:T(8,128)(2,1)}), bf16[64,28,512]{2,1,0:T(8,128)(2,1)S(1)}, u32[]{:S(2)}, u32[]{:S(2)}) async-start(bf16[64,28,512]{2,1,0:T(8,128)(2,1)} %tile.10), calls=%async_computation | async-start | bytes 4194304 | tf_op jit(solution)/shard_map/all_to_all | solution.py:14
  20.6 50.3 %copy-start.9 = (s32[3]{0:T(128)}, s32[3]{0:T(128)S(1)}, u32[]{:S(2)}) copy-start(s32[3]{0:T(128)S(1)} %get-tuple-element.14) | copy-start | bytes 40
  21.9 48.6 %copy-start.11 = (s32[3]{0:T(128)}, s32[3]{0:T(128)S(1)}, u32[]{:S(2)}) copy-start(s32[3]{0:T(128)S(1)} %gather_fusion) | copy-start | bytes 40
  72.4 16.4 %all-to-all-start.1 = ((bf16[64,28,4]{1,2,0:T(4,128)(2,1)}), bf16[64,28,4]{1,2,0:T(4,128)(2,1)S(1)}, u32[]{:S(2)}, u32[]{:S(2)}) async-start(bf16[64,28,4]{1,2,0:T(4,128)(2,1)} %copy.129), calls=%async_computation.1 | async-start | bytes 131072 | tf_op jit(solution)/shard_map/all_to_all | solution.py:81
  88.8 14.8 %all-to-all-start.3 = ((bf16[64,28,4]{1,2,0:T(4,128)(2,1)}), bf16[64,28,4]{1,2,0:T(4,128)(2,1)S(1)}, u32[]{:S(2)}, u32[]{:S(2)}) async-start(bf16[64,28,4]{1,2,0:T(4,128)(2,1)} %copy.150), calls=%async_computation.3 | async-start | bytes 131072 | tf_op jit(solution)/shard_map/all_to_all | solution.py:84
  103.6 10.8 %copy-start.4 = (bf16[1,28,512]{2,1,0:T(8,128)(2,1)S(1)}, bf16[1,28,512]{2,1,0:T(8,128)(2,1)}, u32[]{:S(2)}) copy-start(bf16[1,28,512]{2,1,0:T(8,128)(2,1)} %param.8) | copy-start | bytes 86020
  103.6 10.8 %copy-start.3 = (bf16[1,28,256]{2,1,0:T(8,128)(2,1)S(1)}, bf16[1,28,256]{2,1,0:T(8,128)(2,1)}, u32[]{:S(2)}) copy-start(bf16[1,28,256]{2,1,0:T(8,128)(2,1)} %param.9) | copy-start | bytes 43012
  103.6 10.8 %copy-start.16 = (s32[1,28]{1,0:T(1,128)S(1)}, s32[1,28]{1,0:T(1,128)}, u32[]{:S(2)}) copy-start(s32[1,28]{1,0:T(1,128)} %param.10) | copy-start | bytes 340
  103.6 60.0 %all-to-all-start.2 = ((bf16[64,28,512]{2,1,0:T(8,128)(2,1)}), bf16[64,28,512]{2,1,0:T(8,128)(2,1)S(1)}, u32[]{:S(2)}, u32[]{:S(2)}) async-start(bf16[64,28,512]{2,1,0:T(8,128)(2,1)} %reshape.679), calls=%async_computation.2 | async-start | bytes 4194304 | tf_op jit(solution)/shard_map/all_to_all | solution.py:87
  114.1 137.2 %all-gather.2.cloned.1.call-start = ((), (), s32[]{:S(2)}) async-start(), calls=%async_computation.5 | async-start | bytes 2129920 | tf_op jit(solution)/shard_map/all_gather | solution.py:124
  129.2 37.7 %copy-start.5 = (f32[28,4]{1,0:T(8,128)S(1)}, f32[28,4]{1,0:T(8,128)}, u32[]{:S(2)}) copy-start(f32[28,4]{1,0:T(8,128)} %copy.154) | copy-start | bytes 1348
  129.2 37.8 %copy-start.6 = (f32[28,4]{1,0:T(8,128)S(1)}, f32[28,4]{1,0:T(8,128)}, u32[]{:S(2)}) copy-start(f32[28,4]{1,0:T(8,128)} %copy.148) | copy-start | bytes 1348
  129.2 37.9 %copy-start.7 = (f32[28,4]{1,0:T(8,128)S(1)}, f32[28,4]{1,0:T(8,128)}, u32[]{:S(2)}) copy-start(f32[28,4]{1,0:T(8,128)} %copy.144) | copy-start | bytes 1348
  168.0 127.7 %reduce-scatter.4.cloned.1.call-start = ((), (), s32[]{:S(2)}) async-start(), calls=%async_computation.6 | async-start | bytes 258048
  207.1 49.3 %copy-start.10 = (s32[3]{0:T(128)S(1)}, s32[3]{0:T(128)}, u32[]{:S(2)}) copy-start(s32[3]{0:T(128)} %copy-done.9) | copy-start | bytes 40
  207.1 49.3 %copy-start.12 = (s32[3]{0:T(128)S(1)}, s32[3]{0:T(128)}, u32[]{:S(2)}) copy-start(s32[3]{0:T(128)} %copy-done.11) | copy-start | bytes 40
  256.4 4.3 %copy-start.13 = (pred[3,256]{1,0:T(4,128)(4,1)S(1)}, pred[3,256]{1,0:T(4,128)(4,1)}, u32[]{:S(2)}) copy-start(pred[3,256]{1,0:T(4,128)(4,1)} %get-tuple-element.9) | copy-start | bytes 2308
  256.4 4.4 %copy-start.14 = (pred[3,256]{1,0:T(4,128)(4,1)S(1)}, pred[3,256]{1,0:T(4,128)(4,1)}, u32[]{:S(2)}) copy-start(pred[3,256]{1,0:T(4,128)(4,1)} %get-tuple-element.11) | copy-start | bytes 2308
Sparse Core Ops, SparseCore 0:
  168.1 83.0 all-gather.1
  256.5 39.1 reduce-scatter.3
